TPU v7x, 32 devices: a whole 2x2x4 slice. The times are simulated.
32 devices in a mesh: rep: 4 (over x, core), dom: 8 (over z, y).
Axes of the slice: x: 2, y: 2, z: 4, core: 2. Of those that a mesh axis runs over, the one named last changes fastest.
Arguments:
- coords: float32 [4, 3, 32768], P('rep', None, 'dom'), may hold values from -6 to 6
- atom_var: float32 [32768], P('dom'), may hold values from 0.2 to 1
- atom_weight: float32 [32768], P('dom'), may hold values from 0.5 to 2
- atoms_live: int32 [256], P('dom'), may hold values from 1 to 128, 24576 in all
- block_list: int32 [256, 16], P('dom'), may hold values from 0 to 2047, as said below
- owner_map: int32 [2048], replicated, may hold values from 0 to 2047, as said below
- comp_means: float32 [3, 262144], replicated, may hold values from -6 to 6
- comp_var: float32 [262144], replicated, may hold values from 0.3 to 1.5
- comp_weight: float32 [262144], replicated, may hold values from 0.1 to 1
- target: float32 [262144], P('dom'), may hold values from 0 to 2
- noise_sigma: float32 [262144], P('dom'), may hold values from 0.05 to 0.5
Outputs:
- intersection_avg: float32 [262144], P('dom')
- forces: float32 [4, 3, 32768], P('rep', None, 'dom')
Inputs may be any that keep to these rules, and one draw needn't show every extreme that they name: `atoms_live`: entry a is the number of live atoms of atom block a, held in the first slots of the block. `owner_map`: A permutation of the component blocks. Storage position p lies on dom index p // 256. `block_list`: of the 32 x 16 entries of one dom index's atom blocks, at most 64 name blocks whose storage position lies on any one dom index, and in every draw some dom index receives exactly 64 entries from every dom index. An atom block may list a component block more than once; each entry counts.
All inputs are finite; a program needn't handle non-finite values.
Results may differ from a plain program's by a relative error of at most 0.0003.
Values sent between devices are 32-bit elements; how exact they have to be, the bound alone decides.
A program may use at most 128 MiB of HBM per device.

v0:
```python
import math

import jax
import jax.numpy as jnp
from jax import lax
from jax.sharding import PartitionSpec as P

ATOM_BLK = 128
COMP_BLK = 128
LISTED = 16
BLK_DEV = 32
COMP_BLOCKS = 2048
CAPACITY = 64


full_turn = 2.0 * math.pi
energy_unit = 2.494


def intersection_tile(positions, variances, weights, listed_tile):
    centers = listed_tile[:, 0:3].transpose(1, 0, 2)
    center_var = listed_tile[:, 3]
    center_weight = listed_tile[:, 4]
    offsets = positions[:, None, :, None] - centers[:, :, None, :]
    squared = jnp.sum(offsets * offsets, axis=0)
    widths = variances[None, :, None] + center_var[:, None, :]
    prefactor = weights[None, :, None] * center_weight[:, None, :]
    intersection = prefactor * (full_turn * widths) ** (-1.5) * jnp.exp(-0.5 * squared / widths)
    return (offsets, widths, intersection)


def accumulate(rows, slots, owned):
    picks = (jnp.arange(owned, dtype=jnp.int32)[:, None] == slots.reshape(-1)[None, :]).astype(
        jnp.float32
    )
    return jnp.dot(picks, rows.reshape(-1, COMP_BLK), precision=lax.Precision.HIGHEST)


def shards(
    coords,
    atom_var,
    atom_weight,
    atoms_live,
    block_list,
    owner_map,
    comp_means,
    comp_var,
    comp_weight,
    target,
    noise_sigma,
):
    replicas = lax.axis_size("rep")
    domains = lax.axis_size("dom")
    owned = target.shape[0] // COMP_BLK
    slot_index = jnp.arange(ATOM_BLK, dtype=jnp.int32)
    live_mask = (slot_index[None, :] < atoms_live[:, None]).astype(atom_weight.dtype)
    positions = coords[0].reshape(3, BLK_DEV, ATOM_BLK).transpose(1, 0, 2)
    variances = atom_var.reshape(BLK_DEV, ATOM_BLK)
    weights = atom_weight.reshape(BLK_DEV, ATOM_BLK) * live_mask
    stacked = jnp.concatenate(
        [
            comp_means.reshape(3, COMP_BLOCKS, COMP_BLK).transpose(1, 0, 2),
            comp_var.reshape(COMP_BLOCKS, 1, COMP_BLK),
            comp_weight.reshape(COMP_BLOCKS, 1, COMP_BLK),
        ],
        axis=1,
    )
    listed = stacked[block_list]
    tile_inputs = (positions, variances, weights, listed)

    def tile_of(inputs):
        coord_tile, var_tile, weight_tile, listed_tile = inputs
        return intersection_tile(coord_tile, var_tile, weight_tile, listed_tile)

    def partial_only(inputs):
        offsets, widths, intersection = tile_of(inputs)
        return jnp.sum(intersection, axis=1)

    partials = lax.map(partial_only, tile_inputs)
    entries = BLK_DEV * LISTED
    places = owner_map[block_list].reshape(-1)
    target_dev = places // owned
    target_slot = places % owned
    hits = (target_dev[:, None] == jnp.arange(domains, dtype=jnp.int32)[None, :]).astype(
        jnp.float32
    )
    entry_index = jnp.arange(entries, dtype=jnp.int32)
    lower = (entry_index[:, None] > entry_index[None, :]).astype(jnp.float32)
    before = jnp.dot(lower, hits, precision=lax.Precision.HIGHEST)
    ranks = jnp.sum(before * hits, axis=1).astype(jnp.int32)
    destination = target_dev * CAPACITY + ranks
    placing = (
        jnp.arange(domains * CAPACITY, dtype=jnp.int32)[:, None] == destination[None, :]
    ).astype(jnp.float32)
    send_rows = jnp.dot(
        placing, partials.reshape(entries, COMP_BLK), precision=lax.Precision.HIGHEST
    ).reshape(domains, CAPACITY, COMP_BLK)
    shifted = (target_slot - owned).astype(jnp.float32)[:, None]
    slot_values = jnp.dot(placing, shifted, precision=lax.Precision.HIGHEST)[:, 0] + owned
    send_slots = slot_values.astype(jnp.int32).reshape(domains, CAPACITY)
    got_rows, got_slots = (
        lax.all_to_all(send_rows, "dom", split_axis=0, concat_axis=0, tiled=True),
        lax.all_to_all(send_slots, "dom", split_axis=0, concat_axis=0, tiled=True),
    )
    local_sum = accumulate(got_rows, got_slots, owned)
    summed = lax.psum(local_sum, "rep")
    mean_rows = summed / replicas
    wanted = target.reshape(owned, COMP_BLK)
    sigmas = noise_sigma.reshape(owned, COMP_BLK)
    misfit = mean_rows - wanted
    adjoint = misfit / (sigmas * sigmas + 0.5 * misfit * misfit) / replicas
    padded = jnp.concatenate([adjoint, jnp.zeros((1, COMP_BLK), jnp.float32)], axis=0)
    slot_picks = (
        got_slots.reshape(-1)[:, None] == jnp.arange(owned + 1, dtype=jnp.int32)[None, :]
    ).astype(jnp.float32)
    back_rows = jnp.dot(slot_picks, padded, precision=lax.Precision.HIGHEST).reshape(
        got_slots.shape[0], got_slots.shape[1], COMP_BLK
    )
    returned = lax.all_to_all(back_rows, "dom", split_axis=0, concat_axis=0, tiled=True)
    flat_returned = returned.reshape(domains * CAPACITY, COMP_BLK)
    entry_adjoint = lax.dot_general(
        placing, flat_returned, (((0,), (0,)), ((), ())), precision=lax.Precision.HIGHEST
    ).reshape(BLK_DEV, LISTED, COMP_BLK)

    def force_again(inputs):
        coord_tile, var_tile, weight_tile, listed_tile, adjoint_tile = inputs
        offsets, widths, intersection = tile_of((coord_tile, var_tile, weight_tile, listed_tile))
        weight = adjoint_tile[:, None, :] * (intersection / widths)
        return energy_unit * jnp.sum(weight[None] * offsets, axis=(1, 3))

    forces = lax.map(force_again, (positions, variances, weights, listed, entry_adjoint))
    forces = forces.transpose(1, 0, 2).reshape(3, BLK_DEV * ATOM_BLK)[None]
    return (mean_rows.reshape(-1), forces)


def solution(mesh):
    return jax.shard_map(
        shards,
        mesh=mesh,
        in_specs=(
            P("rep", None, "dom"),
            P("dom"),
            P("dom"),
            P("dom"),
            P("dom", None),
            P(),
            P(),
            P(),
            P(),
            P("dom"),
            P("dom"),
        ),
        out_specs=(P("dom"), P("rep", None, "dom")),
        check_vma=False,
    )
```

profile of v0, /device:TPU:0, one launch (start us, length us, event | category | flops | bytes accessed | tf_op | source)
XLA Modules:
  0.0 265.5 jit_solution(15485615940177351631)
XLA Ops:
  8.1 3.1 %gather_fusion = s32[512]{0:T(512)S(1)} fusion(s32[2048]{0:T(1024)S(1)} %copy-done, s32[1024]{0:T(1024)S(1)} %pad_clamp_fusion), kind=kCustom, calls=%fused_computation | custom fusion | bytes 6144 | tf_op jit(solution)/shard_map/gather | solution.py:81
  12.9 7.3 %all-to-all-start = ((s32[8,1,64]{2,1,0:T(1,128)}), s32[8,1,64]{2,1,0:T(1,128)S(1)}, u32[]{:S(2)}, u32[]{:S(2)}) async-start(s32[8,1,64]{2,1,0:T(1,128)} %bitcast.20), calls=%async_computation | async-start | bytes 8192 | tf_op jit(solution)/shard_map/all_to_all | solution.py:103
  20.3 6.3 %pad_maximum_fusion = f32[2048,5,128]{2,1,0:T(8,128)} fusion(f32[2048,1,128]{2,1,0:T(1,128)S(1)} %bitcast.102, f32[2048,1,128]{2,1,0:T(1,128)S(1)} %bitcast.103, f32[2048,3,128]{2,1,0:T(4,128)} %bitcast.101), kind=kLoop, calls=%fused_computation.43 | loop fusion | flops 2621440 | bytes 10485760 | tf_op jit(solution)/shard_map/concatenate | solution.py:60
  26.6 4.4 %gather_fusion.1 = f32[512,5,128]{2,1,0:T(8,128)S(1)} fusion(f32[2048,5,128]{2,1,0:T(8,128)} %pad_maximum_fusion, s32[1024]{0:T(1024)S(1)} %pad_clamp_fusion), kind=kCustom, calls=%fused_computation.1 | custom fusion | bytes 2623488 | tf_op jit(solution)/shard_map/gather | solution.py:68
  31.4 81.5 %while.20 = (s32[]{:T(128)}, f32[32,16,128]{2,1,0:T(8,128)}, f32[32,128]{1,0:T(8,128)S(1)}, f32[32,16,5,128]{3,1,2,0:T(8,128)S(1)}, f32[32,128]{1,0:T(8,128)}, /*index=5*/f32[32,3,128]{2,1,0:T(4,128)S(1)}, s32[]{:T(128)}) while((s32[]{:T(128)}, f32[32,16,128]{2,1,0:T(8,128)}, f32[32,128]{1,0:T(8,128)S(1)}, f32[32,16,5,128]{3,1,2,0:T(8,128)S(1)}, ...), condition=%wide.region_4.5_spmd, body=%wide.region_1.0_spmd.sunk | while | flops 4192258 | bytes 2334809 | solution.py:79
  37.6 0.8 fusion.51
  40.2 0.8 fusion.51
  42.7 0.8 fusion.51
  45.3 0.8 fusion.51
  60.5 0.8 fusion.51
  63.1 0.8 fusion.51
  65.6 0.8 fusion.51
  68.2 0.8 fusion.51
  70.7 0.8 fusion.51
  75.8 0.8 fusion.51
  78.3 0.8 fusion.51
  80.9 0.8 fusion.51
  83.4 0.8 fusion.51
  86.0 0.8 fusion.51
  91.1 0.8 fusion.51
  93.6 0.8 fusion.51
  96.2 0.8 fusion.51
  112.9 2.3 fusion.16
  115.1 6.0 %all-to-all-start.1 = ((f32[8,64,128]{2,1,0:T(8,128)}), f32[8,64,128]{2,1,0:T(8,128)S(1)}, u32[]{:S(2)}, u32[]{:S(2)}) async-start(f32[8,64,128]{2,1,0:T(8,128)} %fusion.16), calls=%async_computation.1 | async-start | bytes 524288 | tf_op jit(solution)/shard_map/all_to_all | solution.py:102
  122.4 7.2 %all-to-all-done.1 = f32[8,64,128]{2,1,0:T(8,128)S(1)} async-done(((f32[8,64,128]{2,1,0:T(8,128)}), f32[8,64,128]{2,1,0:T(8,128)S(1)}, u32[]{:S(2)}, u32[]{:S(2)}) %all-to-all-start.1) | async-done | bytes 262176 | tf_op jit(solution)/shard_map/all_to_all | solution.py:102
  129.6 1.1 fusion.26
  130.7 30.8 %all-reduce.3.cloned.1.call-done = f32[256,128]{1,0:T(8,128)} async-done(((f32[256,128]{1,0:T(8,128)}), f32[256,128]{1,0:T(8,128)}) %all-reduce.3.cloned.1.call-update) | async-done | bytes 131088 | tf_op jit(solution)/shard_map/psum | solution.py:106
  161.5 1.6 fusion.32
  163.1 1.2 fusion.21
  164.3 5.5 %all-to-all-start.2 = ((f32[8,64,128]{2,1,0:T(8,128)}), f32[8,64,128]{2,1,0:T(8,128)S(1)}, u32[]{:S(2)}, u32[]{:S(2)}) async-start(f32[8,64,128]{2,1,0:T(8,128)} %bitcast.37), calls=%async_computation.2 | async-start | bytes 524288 | tf_op jit(solution)/shard_map/all_to_all | solution.py:119
  170.1 8.0 %all-to-all-done.2 = f32[8,64,128]{2,1,0:T(8,128)S(1)} async-done(((f32[8,64,128]{2,1,0:T(8,128)}), f32[8,64,128]{2,1,0:T(8,128)S(1)}, u32[]{:S(2)}, u32[]{:S(2)}) %all-to-all-start.2) | async-done | bytes 262176 | tf_op jit(solution)/shard_map/all_to_all | solution.py:119
  178.7 79.4 %while.21 = (s32[]{:T(128)}, f32[32,3,128]{2,1,0:T(4,128)S(1)}, f32[32,16,128]{2,1,0:T(8,128)S(1)}, f32[32,128]{1,0:T(8,128)S(1)}, f32[32,16,5,128]{3,1,2,0:T(8,...) while((s32[]{:T(128)}, f32[32,3,128]{2,1,0:T(4,128)S(1)}, ...), condition=%wide.region_9.10_spmd, body=%wide.region_6.9_spmd.sunk | while | flops 6815746 | bytes 4463209 | solution.py:131
  179.8 0.8 fusion.54
  182.3 0.8 fusion.54
  184.8 0.8 fusion.54
  187.3 0.8 fusion.54
  189.8 0.8 fusion.54
  192.2 0.8 fusion.54
  194.7 0.8 fusion.54
  197.2 0.8 fusion.54
  199.7 0.8 fusion.54
  202.2 0.8 fusion.54
  204.6 0.8 fusion.54
  207.1 0.8 fusion.54
  209.6 0.8 fusion.54
  212.1 0.8 fusion.54
  214.6 0.8 fusion.54
  217.0 0.8 fusion.54
  219.5 0.8 fusion.54
  222.0 0.8 fusion.54
  224.5 0.8 fusion.54
  227.0 0.8 fusion.54
  229.4 0.8 fusion.54
  231.9 0.8 fusion.54
  234.4 0.8 fusion.54
  236.9 0.8 fusion.54
  239.4 0.8 fusion.54
  241.8 0.8 fusion.54
  244.3 0.8 fusion.54
  246.8 0.8 fusion.54
  249.3 0.8 fusion.54
  251.8 0.8 fusion.54
  254.2 0.8 fusion.54
  256.7 0.8 fusion.54
  (567 shorter events, 123.7 us)
Async XLA Ops:
  7.2 0.9 copy-start
  8.1 12.2 %copy-start.1 = (f32[262144]{0:T(1024)S(1)}, f32[262144]{0:T(1024)}, u32[]{:S(2)}) copy-start(f32[262144]{0:T(1024)} %param.23) | copy-start | bytes 3145732
  8.1 12.2 %copy-start.2 = (f32[262144]{0:T(1024)S(1)}, f32[262144]{0:T(1024)}, u32[]{:S(2)}) copy-start(f32[262144]{0:T(1024)} %param.22) | copy-start | bytes 3145732
  12.9 102.2 %all-to-all-start = ((s32[8,1,64]{2,1,0:T(1,128)}), s32[8,1,64]{2,1,0:T(1,128)S(1)}, u32[]{:S(2)}, u32[]{:S(2)}) async-start(s32[8,1,64]{2,1,0:T(1,128)} %bitcast.20), calls=%async_computation | async-start | bytes 8192 | tf_op jit(solution)/shard_map/all_to_all | solution.py:103
  26.6 4.6 %copy-start.5 = (f32[1,3,4096]{2,0,1:T(1,128)S(1)}, f32[1,3,4096]{2,0,1:T(1,128)}, u32[]{:S(2)}) copy-start(f32[1,3,4096]{2,0,1:T(1,128)} %param.15) | copy-start | bytes 147460
  26.6 4.7 %copy-start.6 = (f32[4096]{0:T(1024)S(1)}, f32[4096]{0:T(1024)}, u32[]{:S(2)}) copy-start(f32[4096]{0:T(1024)} %param.17) | copy-start | bytes 49156
  26.6 4.7 %copy-start.7 = (s32[32]{0:T(128)S(1)}, s32[32]{0:T(128)}, u32[]{:S(2)}) copy-start(s32[32]{0:T(128)} %param.18) | copy-start | bytes 388
  31.4 130.1 %copy-start.3 = (f32[32768]{0:T(1024)S(1)}, f32[32768]{0:T(1024)}, u32[]{:S(2)}) copy-start(f32[32768]{0:T(1024)} %param.24) | copy-start | bytes 393220
  31.4 130.1 %copy-start.4 = (f32[32768]{0:T(1024)S(1)}, f32[32768]{0:T(1024)}, u32[]{:S(2)}) copy-start(f32[32768]{0:T(1024)} %param.25) | copy-start | bytes 393220
  115.1 14.5 %all-to-all-start.1 = ((f32[8,64,128]{2,1,0:T(8,128)}), f32[8,64,128]{2,1,0:T(8,128)S(1)}, u32[]{:S(2)}, u32[]{:S(2)}) async-start(f32[8,64,128]{2,1,0:T(8,128)} %fusion.16), calls=%async_computation.1 | async-start | bytes 524288 | tf_op jit(solution)/shard_map/all_to_all | solution.py:102
  121.1 40.4 %all-reduce.3.cloned.1.call-start = ((), (), s32[]{:S(2)}) async-start(), calls=%async_computation.3 | async-start | bytes 262144 | tf_op jit(solution)/shard_map/psum | solution.py:106
  164.3 13.7 %all-to-all-start.2 = ((f32[8,64,128]{2,1,0:T(8,128)}), f32[8,64,128]{2,1,0:T(8,128)S(1)}, u32[]{:S(2)}, u32[]{:S(2)}) async-start(f32[8,64,128]{2,1,0:T(8,128)} %bitcast.37), calls=%async_computation.2 | async-start | bytes 524288 | tf_op jit(solution)/shard_map/all_to_all | solution.py:119
Sparse Core Ops, SparseCore 0:
  130.8 30.6 all-reduce.2
where the time goes:
time: 268 us; the launch traced here: 265 us
  other arithmetic  103 us (38%)
  local copies, waits for them, and re-layouts  74.6 us (28%)
  waiting for transfers between devices  46 us (17%)
  starting transfers between devices  18.9 us (7%)
  between operations  14.2 us (5%)
  matrix products  6.15 us (2%)
  loops' own time  2.8 us (1%)
    mul x128, local copies, waits for them, and re-layouts, intersection_tile(): prefactor = weights[None, :, None] * center_weight[:, None, :]  45 us
    psum x1, waiting for transfers between devices, shards(): summed = lax.psum(local_sum, 'rep')  30.8 us
    mul x32, other arithmetic, force_again(): weight = adjoint_tile[:, None, :] * (intersection / widths)  26.3 us
    reduce_sum x32, other arithmetic, partial_only(): return jnp.sum(intersection, axis=1)  26 us
    reduce_sum x64, other arithmetic, intersection_tile(): squared = jnp.sum(offsets * offsets, axis=0)  25.3 us
    dynamic_update_slice x32, local copies, waits for them, and re-layouts, shards(): partials = lax.map(partial_only, tile_inputs)  19.2 us
    reduce_sum x32, other arithmetic, force_again(): return energy_unit * jnp.sum(weight[None] * offsets, axis=(1, 3))  14.7 us
    all_to_all x1, waiting for transfers between devices, shards(): lax.all_to_all(back_rows, 'dom', split_axis=0, concat_axis=0, tiled=True)  8 us
  transfers between devices with their start and end apart: 4, of which 3 were waited for; matrix products, arithmetic and copies ran while one was open for 36% of the time, Pallas kernels for 0%

commit v1 on v0

v1 whole, which is shorter than its diff:
```python
import functools
import math

import jax
import jax.numpy as jnp
from jax import lax
from jax.experimental import pallas as pl
from jax.experimental.pallas import tpu as pltpu
from jax.sharding import PartitionSpec as P

CAPACITY = 64
ROWS = CAPACITY + 8
LANES = 128
SUB = 32

energy_unit = 2.494
norm = (2.0 * math.pi) ** -1.5
half_log2e = -0.5 / math.log(2.0)
VMEM = pltpu.VMEM
MESH = pl.DeviceIdType.MESH


def three(value):
    first = value.astype(jnp.bfloat16)
    rest = value - first.astype(jnp.float32)
    second = rest.astype(jnp.bfloat16)
    third = (rest - second.astype(jnp.float32)).astype(jnp.bfloat16)
    return first, second, third


def three_f32(value):
    return [piece.astype(jnp.float32) for piece in three(value)]


def pair_kernel(
    listed, owned, live, lst, owner, x_ref, av_ref, aw_ref, m_ref, cv_ref, cw_ref,
    send_ref, pos_ref, g_ref, count, avb, wb,
):
    a = pl.program_id(0)
    domains = send_ref.shape[0]

    @pl.when(a == 0)
    def _():
        send_ref[...] = jnp.zeros_like(send_ref)
        send_ref[:, CAPACITY : CAPACITY + 8, :] = jnp.full((domains, 8, LANES), -1.0, jnp.float32)
        for d in range(domains):
            count[d] = 0

    x = x_ref[...]
    lane = lax.broadcasted_iota(jnp.int32, (1, LANES), 1)
    weights = jnp.where(lane < live[a], aw_ref[0], 0.0)
    avb[...] = jnp.transpose(jnp.broadcast_to(av_ref[0], (LANES, LANES)))
    wb[...] = jnp.transpose(jnp.broadcast_to(weights, (LANES, LANES)))
    xx = jnp.sum(x * x, axis=0, keepdims=True)
    left = half_log2e * jnp.concatenate(
        [-2.0 * x, jnp.ones((1, LANES), jnp.float32), xx, jnp.zeros((3, LANES), jnp.float32)], axis=0
    )
    l0, l1, l2 = three_f32(left)
    lhs = jnp.concatenate([l0, l0, l1, l1, l0, l2], axis=0).astype(jnp.bfloat16)
    for k in range(listed):
        b = lst[a * listed + k]
        m = m_ref[:, pl.ds(pl.multiple_of(b * LANES, LANES), LANES)]
        mm = jnp.sum(m * m, axis=0, keepdims=True)
        right = jnp.concatenate(
            [m, mm, jnp.ones((1, LANES), jnp.float32), jnp.zeros((3, LANES), jnp.float32)], axis=0
        )
        r0, r1, r2 = three_f32(right)
        rhs = jnp.concatenate([r0, r1, r0, r1, r2, r0], axis=0).astype(jnp.bfloat16)
        scaled = lax.dot_general(
            lhs, rhs, (((0,), (0,)), ((), ())), preferred_element_type=jnp.float32
        )
        cv = cv_ref[pl.ds(b, 1), :]
        total = jnp.zeros((SUB, LANES), jnp.float32)
        for h in range(LANES // SUB):
            rows = slice(h * SUB, (h + 1) * SUB)
            root = lax.rsqrt(avb[rows, :] + cv)
            inv = root * root
            ov = (root * inv) * jnp.exp2(scaled[rows] * inv) * wb[rows, :]
            g_ref[k * LANES + h * SUB : k * LANES + (h + 1) * SUB, :] = ov * inv
            total = total + ov
        partial = jnp.sum(total, axis=0, keepdims=True) * (norm * cw_ref[pl.ds(b, 1), :])
        place = owner[b]
        dev = lax.div(place, owned)
        slot = place - dev * owned
        rank = count[dev]
        count[dev] = rank + 1
        pos_ref[a * listed + k] = dev * CAPACITY + rank
        send_ref[dev, pl.ds(rank, 1), :] = partial
        before = send_ref[dev, CAPACITY : CAPACITY + 1, :]
        send_ref[dev, CAPACITY : CAPACITY + 1, :] = jnp.where(
            lane == rank, slot.astype(jnp.float32), before
        )


def force_kernel(listed, pos, lst, x_ref, g_ref, ret_ref, m_ref, cw_ref, f_ref, coef, sums):
    a = pl.program_id(0)
    for k in range(listed):
        b = lst[a * listed + k]
        adj = ret_ref[pl.ds(pos[a * listed + k], 1), :]
        scale = adj * (cw_ref[pl.ds(b, 1), :] * (energy_unit * norm))
        m = m_ref[:, pl.ds(pl.multiple_of(b * LANES, LANES), LANES)]
        coef[k, 0] = jnp.broadcast_to(scale, (8, LANES))
        for c in range(3):
            coef[k, c + 1] = jnp.broadcast_to(scale * m[c : c + 1], (8, LANES))
    step = 16
    for h in range(LANES // step):
        acc = [jnp.zeros((step // 8, 8, LANES), jnp.float32) for _ in range(4)]
        for k in range(listed):
            g = g_ref[k * LANES + h * step : k * LANES + (h + 1) * step, :].reshape(
                step // 8, 8, LANES
            )
            for c in range(4):
                acc[c] = acc[c] + g * coef[k, c][None]
        for c in range(4):
            sums[c, h * step : (h + 1) * step, :] = acc[c].reshape(step, LANES)
    ones = jnp.ones((8, LANES), jnp.float32)
    flat = [
        lax.dot_general(
            ones, sums[c], (((1,), (1,)), ((), ())), precision=lax.Precision.HIGHEST,
            preferred_element_type=jnp.float32,
        )[0:1]
        for c in range(4)
    ]
    for c in range(3):
        f_ref[c : c + 1, :] = x_ref[c : c + 1, :] * flat[0] - flat[c + 1]


def exchange_kernel(
    domains, replicas, send_ref, target_ref, sigma_ref, mean_ref, ret_ref,
    got, acc, part, back, land, out_send, out_recv, rep_send, rep_recv, back_send, back_recv,
):
    me_d = lax.axis_index("dom")
    me_r = lax.axis_index("rep")
    owned = target_ref.shape[0]
    stages = replicas.bit_length() - 1
    partners = []
    for t in range(stages):
        bit = 1 << t
        partners.append(me_r + bit - 2 * bit * lax.rem(lax.div(me_r, bit), 2))
    barrier = pltpu.get_barrier_semaphore()
    for s in range(1, domains):
        pl.semaphore_signal(
            barrier, inc=1, device_id=(me_r, lax.rem(me_d + s, domains)), device_id_type=MESH
        )
    for t in range(stages):
        pl.semaphore_signal(barrier, inc=1, device_id=(partners[t], me_d), device_id_type=MESH)
    pl.semaphore_wait(barrier, domains - 1 + stages)

    outs = [None]
    for s in range(1, domains):
        peer = lax.rem(me_d + s, domains)
        copy = pltpu.make_async_remote_copy(
            src_ref=send_ref.at[peer],
            dst_ref=got.at[s],
            send_sem=out_send.at[s],
            recv_sem=out_recv.at[s],
            device_id=(me_r, peer),
            device_id_type=MESH,
        )
        copy.start()
        outs.append(copy)

    row = lax.broadcasted_iota(jnp.int32, (owned, CAPACITY), 0).astype(jnp.float32)

    def picks_of(s):
        slots = (
            send_ref[me_d, CAPACITY : CAPACITY + 1, :] if s == 0 else got[s, CAPACITY : CAPACITY + 1, :]
        )
        return jnp.where(row == slots[:, :CAPACITY], 1.0, 0.0).astype(jnp.bfloat16)

    total = jnp.zeros((owned, LANES), jnp.float32)
    for s in range(domains):
        if s:
            outs[s].wait_recv()
        rows = send_ref[me_d, :CAPACITY, :] if s == 0 else got[s, :CAPACITY, :]
        picks = picks_of(s)
        for piece in three(rows):
            total = total + jnp.dot(picks, piece, preferred_element_type=jnp.float32)
    acc[0] = total
    swaps = []
    for t in range(stages):
        copy = pltpu.make_async_remote_copy(
            src_ref=acc.at[t],
            dst_ref=part.at[t],
            send_sem=rep_send.at[t],
            recv_sem=rep_recv.at[t],
            device_id=(partners[t], me_d),
            device_id_type=MESH,
        )
        copy.start()
        swaps.append(copy)
        copy.wait_recv()
        total = total + part[t]
        if t + 1 < stages:
            acc[t + 1] = total
    mean = total / replicas
    mean_ref[...] = mean
    misfit = mean - target_ref[...]
    sigmas = sigma_ref[...]
    adjoint = misfit / (sigmas * sigmas + 0.5 * misfit * misfit) / replicas
    pieces = three(adjoint)
    backs = []
    for s in list(range(1, domains)) + [0]:
        picks = picks_of(s)
        rows = jnp.zeros((CAPACITY, LANES), jnp.float32)
        for piece in pieces:
            rows = rows + lax.dot_general(
                picks, piece, (((0,), (0,)), ((), ())), preferred_element_type=jnp.float32
            )
        if s == 0:
            ret_ref[me_d] = rows
            continue
        back[s] = rows
        peer = lax.rem(me_d + domains - s, domains)
        copy = pltpu.make_async_remote_copy(
            src_ref=back.at[s],
            dst_ref=land.at[s],
            send_sem=back_send.at[s],
            recv_sem=back_recv.at[s],
            device_id=(me_r, peer),
            device_id_type=MESH,
        )
        copy.start()
        backs.append((s, copy))
    for s, copy in backs:
        copy.wait_recv()
        ret_ref[lax.rem(me_d + s, domains)] = land[s]
    for copy in outs[1:] + swaps + [copy for _, copy in backs]:
        copy.wait_send()


def shards(
    coords, atom_var, atom_weight, atoms_live, block_list, owner_map,
    comp_means, comp_var, comp_weight, target, noise_sigma,
):
    replicas = lax.axis_size("rep")
    domains = lax.axis_size("dom")
    blocks, listed = block_list.shape
    comp_blocks = owner_map.shape[0]
    owned = target.shape[0] // LANES
    entries = blocks * listed
    x = coords[0]
    lst = block_list.reshape(-1)
    cv = comp_var.reshape(comp_blocks, LANES)
    cw = comp_weight.reshape(comp_blocks, LANES)
    whole = pl.BlockSpec(memory_space=VMEM)
    per_block = pl.BlockSpec((1, 1, LANES), lambda a, *_: (a, 0, 0))
    x_spec = pl.BlockSpec((3, LANES), lambda a, *_: (0, a))
    g_spec = pl.BlockSpec((listed * LANES, LANES), lambda a, *_: (a, 0))
    send, pos, g = pl.pallas_call(
        functools.partial(pair_kernel, listed, owned),
        grid_spec=pltpu.PrefetchScalarGridSpec(
            num_scalar_prefetch=3,
            grid=(blocks,),
            in_specs=[x_spec, per_block, per_block, whole, whole, whole],
            out_specs=[whole, pl.BlockSpec(memory_space=pltpu.SMEM), g_spec],
            scratch_shapes=[
                pltpu.SMEM((domains,), jnp.int32),
                VMEM((LANES, LANES), jnp.float32),
                VMEM((LANES, LANES), jnp.float32),
            ],
        ),
        out_shape=[
            jax.ShapeDtypeStruct((domains, ROWS, LANES), jnp.float32),
            jax.ShapeDtypeStruct((entries,), jnp.int32),
            jax.ShapeDtypeStruct((entries * LANES, LANES), jnp.float32),
        ],
        compiler_params=pltpu.CompilerParams(vmem_limit_bytes=40 << 20),
        name="pairs",
    )(
        atoms_live, lst, owner_map, x,
        atom_var.reshape(blocks, 1, LANES), atom_weight.reshape(blocks, 1, LANES),
        comp_means, cv, cw,
    )
    stages = replicas.bit_length() - 1
    mean, ret = pl.pallas_call(
        functools.partial(exchange_kernel, domains, replicas),
        in_specs=[whole] * 3,
        out_specs=[whole] * 2,
        out_shape=[
            jax.ShapeDtypeStruct((owned, LANES), jnp.float32),
            jax.ShapeDtypeStruct((domains, CAPACITY, LANES), jnp.float32),
        ],
        scratch_shapes=[
            VMEM((domains, ROWS, LANES), jnp.float32),
            VMEM((stages, owned, LANES), jnp.float32),
            VMEM((stages, owned, LANES), jnp.float32),
            VMEM((domains, CAPACITY, LANES), jnp.float32),
            VMEM((domains, CAPACITY, LANES), jnp.float32),
            pltpu.SemaphoreType.DMA((domains,)),
            pltpu.SemaphoreType.DMA((domains,)),
            pltpu.SemaphoreType.DMA((stages,)),
            pltpu.SemaphoreType.DMA((stages,)),
            pltpu.SemaphoreType.DMA((domains,)),
            pltpu.SemaphoreType.DMA((domains,)),
        ],
        compiler_params=pltpu.CompilerParams(
            collective_id=0, has_side_effects=True, vmem_limit_bytes=24 << 20
        ),
        name="exchange",
    )(send, target.reshape(owned, LANES), noise_sigma.reshape(owned, LANES))
    forces = pl.pallas_call(
        functools.partial(force_kernel, listed),
        grid_spec=pltpu.PrefetchScalarGridSpec(
            num_scalar_prefetch=2,
            grid=(blocks,),
            in_specs=[x_spec, g_spec, whole, whole, whole],
            out_specs=x_spec,
            scratch_shapes=[
                VMEM((listed, 4, 8, LANES), jnp.float32),
                VMEM((4, LANES, LANES), jnp.float32),
            ],
        ),
        out_shape=jax.ShapeDtypeStruct((3, blocks * LANES), jnp.float32),
        compiler_params=pltpu.CompilerParams(vmem_limit_bytes=40 << 20),
        name="forces",
    )(pos, lst, x, g, ret.reshape(domains * CAPACITY, LANES), comp_means, cw)
    return (mean.reshape(-1), forces[None])


def solution(mesh):
    return jax.shard_map(
        shards,
        mesh=mesh,
        in_specs=(
            P("rep", None, "dom"),
            P("dom"),
            P("dom"),
            P("dom"),
            P("dom", None),
            P(),
            P(),
            P(),
            P(),
            P("dom"),
            P("dom"),
        ),
        out_specs=(P("dom"), P("rep", None, "dom")),
        check_vma=False,
    )
```

time: 268 us -> 106 us (0.40)
  other arithmetic: 103 us -> 0 us
  Pallas kernels: 0 us -> 88.6 us
  local copies, waits for them, and re-layouts: 74.6 us -> 15.7 us
  waiting for transfers between devices: 46 us -> 0 us
  starting transfers between devices: 18.9 us -> 0 us
  between operations: 14.2 us -> 0.67 us
  matrix products: 6.15 us -> 0 us
  loops' own time: 2.8 us -> 0 us
    pallas_call x0 -> x3, Pallas kernels: none -> 88.6 us  [the longest x1 33.5 us: shards(): pl.pallas_call(functools.partial(force_kernel, listed), grid_spec=pltpu.P...]
    reduce_sum x128 -> x0, other arithmetic: 66 us -> none  [the longest x32 26 us: partial_only(): return jnp.sum(intersection, axis=1)]
    mul x160 -> x0, local copies, waits for them, and re-layouts: 45.1 us -> none  [the longest x128 45 us: intersection_tile(): prefactor = weights[None, :, None] * center_weight[:, None, :]]
    psum x1 -> x0, waiting for transfers between devices: 30.8 us -> none  [shards(): summed = lax.psum(local_sum, 'rep')]
    mul x33 -> x0, other arithmetic: 26.3 us -> none  [the longest x32 26.3 us: force_again(): weight = adjoint_tile[:, None, :] * (intersection / widths)]
    dynamic_update_slice x32 -> x0, local copies, waits for them, and re-layouts: 19.2 us -> none  [shards(): partials = lax.map(partial_only, tile_inputs)]
    all_to_all x3 -> x0, starting transfers between devices: 18.8 us -> none  [the longest x1 7.31 us: shards(): lax.all_to_all(send_slots, 'dom', split_axis=0, concat_axis=0, tiled=True)]
    unnamed x16 -> x26, local copies, waits for them, and re-layouts: 0.04 us -> 15.6 us
  transfers between devices with their start and end apart: 4 -> 0, of which waited for: 3 -> 0; matrix products, arithmetic and copies ran while one was open for 36% -> 0% of each run, Pallas kernels for 0% -> 0%
where the time goes in v1:
time: 106 us; the launch traced here: 105 us
  Pallas kernels  88.6 us (84%)
  local copies, waits for them, and re-layouts  15.7 us (15%)
    pallas_call x1, Pallas kernels, shards(): pl.pallas_call(functools.partial(force_kernel, listed), grid_spec=pltpu.P...  33.5 us
    pallas_call x1, Pallas kernels, shards(): pl.pallas_call(functools.partial(exchange_kernel, domains, replicas), in_...  28.6 us
    pallas_call x1, Pallas kernels, shards(): pl.pallas_call(functools.partial(pair_kernel, listed, owned), grid_spec=p...  26.5 us
    unnamed x26, local copies, waits for them, and re-layouts  15.6 us

profile of v1, /device:TPU:0, one launch (start us, length us, event | category | flops | bytes accessed | tf_op | source)
XLA Modules:
  0.0 105.0 jit_solution(11630044971959160256)
XLA Ops:
  0.6 0.8 copy.14
  1.4 0.1 reshape.31.lst
  1.5 0.8 copy.18
  2.3 0.0 copy-start
  2.3 2.2 %copy-done = f32[3,262144]{1,0:T(4,128)S(1)} copy-done((f32[3,262144]{1,0:T(4,128)S(1)}, f32[3,262144]{1,0:T(4,128)}, u32[]{:S(2)}) %copy-start) | copy-done | bytes 3145752
  4.5 0.0 copy-start.2
  4.5 1.2 %copy-done.2 = f32[262144]{0:T(1024)S(1)} copy-done((f32[262144]{0:T(1024)S(1)}, f32[262144]{0:T(1024)}, u32[]{:S(2)}) %copy-start.2) | copy-done | bytes 1048600
  5.7 0.0 copy-start.4
  5.7 1.2 %copy-done.4 = f32[262144]{0:T(1024)S(1)} copy-done((f32[262144]{0:T(1024)S(1)}, f32[262144]{0:T(1024)}, u32[]{:S(2)}) %copy-start.4) | copy-done | bytes 1048600
  7.0 0.0 copy-start.7
  7.0 0.7 copy-done.7
  7.7 0.0 copy-start.8
  7.7 0.7 copy-done.8
  8.4 0.0 copy-start.9
  8.4 0.7 copy-done.9
  9.1 0.0 copy-start.10
  9.1 0.7 copy-done.10
  9.8 26.5 %pairs.1 = (f32[8,72,128]{2,1,0:T(8,128)S(1)}, s32[512]{0:T(512)S(1)}, f32[65536,128]{1,0:T(8,128)}) custom-call(s32[32]{0:T(128)S(1)} %copy-done.10, s32[512]{0:T(512)S(1)} %reshape.31.lst, s32[2048]{0:T(1024)S(1)} %copy-done.9, f32[3,4096]{1,0:T(4,128)S(1)} %bitcast.15, f32[32,1,128]{2,1,0:T(1,128)S(1)} %bitcast.22, f32[32,1,128]{2,1,0:T(1,128)S(1)} %bitcast.23, ...), custom_call_target="tpu_custom_call" | custom-call | tf_op jit(solution)/shard_map/pairs/pallas_call | solution.py:250
  36.3 0.0 copy-start.5
  36.3 0.9 copy-done.5
  37.2 0.0 copy-start.6
  37.2 0.9 copy-done.6
  38.1 28.6 %exchange.1 = (f32[256,128]{1,0:T(8,128)S(1)}, f32[8,64,128]{2,1,0:T(8,128)S(1)}) custom-call(f32[8,72,128]{2,1,0:T(8,128)S(1)} %get-tuple-element.7.send_ref, f32[256,128]{1,0:T(8,128)S(1)} %bitcast.19, f32[256,128]{1,0:T(8,128)S(1)} %bitcast.20), custom_call_target="tpu_custom_call" | custom-call | tf_op jit(solution)/shard_map/exchange/pallas_call | solution.py:276
  66.7 0.0 copy-start.1
  66.7 2.2 %copy-done.1 = f32[3,262144]{1,0:T(4,128)S(1)} copy-done((f32[3,262144]{1,0:T(4,128)S(1)}, f32[3,262144]{1,0:T(4,128)}, u32[]{:S(2)}) %copy-start.1) | copy-done | bytes 3145752
  68.9 0.0 copy-start.3
  68.9 1.2 %copy-done.3 = f32[262144]{0:T(1024)S(1)} copy-done((f32[262144]{0:T(1024)S(1)}, f32[262144]{0:T(1024)}, u32[]{:S(2)}) %copy-start.3) | copy-done | bytes 1048600
  70.1 33.5 %forces.1 = f32[3,4096]{1,0:T(4,128)S(1)} custom-call(s32[512]{0:T(512)S(1)} %get-tuple-element.9.pos, s32[512]{0:T(512)S(1)} %reshape.31.lst, f32[3,4096]{1,0:T(4,128)S(1)} %bitcast.16, f32[65536,128]{1,0:T(8,128)} %get-tuple-element.10.g_ref, f32[512,128]{1,0:T(8,128)S(1)} %bitcast.17, f32[3,262144]{1,0:T(4,128)S(1)} %copy-done.1, f32[2048,128]{1,0:T(8,128)S(1)} %bitcast.13), custom_call_target="tpu_custom_call" | custom-call | tf_op jit(solution)/shard_map/forces/pallas_call | solution.py:302
  103.6 0.7 copy.15
  104.3 0.7 copy.20
Async XLA Ops:
  2.3 2.2 %copy-start = (f32[3,262144]{1,0:T(4,128)S(1)}, f32[3,262144]{1,0:T(4,128)}, u32[]{:S(2)}) copy-start(f32[3,262144]{1,0:T(4,128)} %m_ref.3) | copy-start | bytes 9437188
  4.5 1.2 %copy-start.2 = (f32[262144]{0:T(1024)S(1)}, f32[262144]{0:T(1024)}, u32[]{:S(2)}) copy-start(f32[262144]{0:T(1024)} %param.19) | copy-start | bytes 3145732
  5.7 1.2 %copy-start.4 = (f32[262144]{0:T(1024)S(1)}, f32[262144]{0:T(1024)}, u32[]{:S(2)}) copy-start(f32[262144]{0:T(1024)} %param.18) | copy-start | bytes 3145732
  7.0 0.7 copy-start.7
  7.7 0.7 copy-start.8
  8.4 0.7 copy-start.9
  9.1 0.7 copy-start.10
  36.3 0.9 copy-start.5
  37.2 0.9 copy-start.6
  66.7 2.2 %copy-start.1 = (f32[3,262144]{1,0:T(4,128)S(1)}, f32[3,262144]{1,0:T(4,128)}, u32[]{:S(2)}) copy-start(f32[3,262144]{1,0:T(4,128)} %m_ref.3) | copy-start | bytes 9437188
  68.9 1.2 %copy-start.3 = (f32[262144]{0:T(1024)S(1)}, f32[262144]{0:T(1024)}, u32[]{:S(2)}) copy-start(f32[262144]{0:T(1024)} %param.19) | copy-start | bytes 3145732

commit v2 on v1

v2 whole, which is shorter than its diff:
```python
import functools
import math

import jax
import jax.numpy as jnp
from jax import lax
from jax.experimental import pallas as pl
from jax.experimental.pallas import tpu as pltpu
from jax.sharding import PartitionSpec as P

CAPACITY = 64
ROWS = CAPACITY + 8
LANES = 128
SUB = 32
OUT_SLOTS = 3
IN_SLOTS = 5

energy_unit = 2.494
norm = (2.0 * math.pi) ** -1.5
half_log2e = -0.5 / math.log(2.0)
VMEM = pltpu.VMEM
MESH = pl.DeviceIdType.MESH


def three(value):
    first = value.astype(jnp.bfloat16)
    rest = value - first.astype(jnp.float32)
    second = rest.astype(jnp.bfloat16)
    third = (rest - second.astype(jnp.float32)).astype(jnp.bfloat16)
    return first, second, third


def three_f32(value):
    return [piece.astype(jnp.float32) for piece in three(value)]


def pair_kernel(
    listed, owned, live_h, lst_h, owner_h, x_h, av_h, aw_h, m_h, cv_h, cw_h,
    send_ref, pos_ref, table_ref, g_h,
    g_buf, g_sems, live, lst, owner, x_v, av_v, aw_v, m_v, cv_v, cw_v, count, avb, wb, lhs_s, rhs_s, cvs, sums, sems,
):
    domains = send_ref.shape[0]
    blocks = live.shape[0]
    loads = [
        pltpu.make_async_copy(src, dst, sems.at[i])
        for i, (src, dst) in enumerate(
            [(m_h, m_v), (cv_h, cv_v), (cw_h, cw_v), (x_h, x_v), (av_h, av_v), (aw_h, aw_v),
             (owner_h, owner), (lst_h, lst), (live_h, live)]
        )
    ]
    for load in loads:
        load.start()
    send_ref[...] = jnp.zeros_like(send_ref)
    send_ref[:, CAPACITY : CAPACITY + 8, :] = jnp.full((domains, 8, LANES), -1.0, jnp.float32)
    for d in range(domains):
        count[d] = 0
    for load in loads:
        load.wait()
    lane = lax.broadcasted_iota(jnp.int32, (1, LANES), 1)
    one = jnp.ones((1, LANES), jnp.float32)
    none = jnp.zeros((3, LANES), jnp.float32)

    def out_copy(a, h):
        turn = lax.rem(a, OUT_SLOTS)
        return pltpu.make_async_copy(g_buf.at[turn, h], g_h.at[a, h], g_sems.at[turn, h])

    def drain(a):
        for h in range(LANES // SUB):

            @pl.when(live[a] > h * SUB)
            def _():
                out_copy(a, h).wait()

    def block(a, carry):
        n_live = live[a]
        turn = lax.rem(a, OUT_SLOTS)

        @pl.when(a >= OUT_SLOTS)
        def _():
            drain(a - OUT_SLOTS)

        x = jnp.concatenate(
            [x_v[c, :, pl.ds(pl.multiple_of(a * LANES, LANES), LANES)] for c in range(3)], axis=0
        )
        weights = jnp.where(lane < n_live, aw_v[pl.ds(a, 1), :], 0.0)
        avb[...] = jnp.transpose(jnp.broadcast_to(av_v[pl.ds(a, 1), :], (LANES, LANES)))
        wb[...] = jnp.transpose(jnp.broadcast_to(weights, (LANES, LANES)))
        xx = jnp.sum(x * x, axis=0, keepdims=True)
        left = half_log2e * jnp.concatenate([-2.0 * x, one, xx, none], axis=0)
        l0, l1, l2 = three_f32(left)
        pad = jnp.zeros((LANES - 48, LANES), jnp.float32)
        lhs_s[...] = jnp.transpose(jnp.concatenate([l0, l0, l1, l1, l0, l2, pad], axis=0)).astype(
            jnp.bfloat16
        )
        for k in range(listed):
            e = a * listed + k
            b = lst[e]
            m = m_v[:, pl.ds(pl.multiple_of(b * LANES, LANES), LANES)]
            mm = jnp.sum(m * m, axis=0, keepdims=True)
            r0, r1, r2 = three_f32(jnp.concatenate([m, mm, one, none], axis=0))
            rhs_s[:, k * LANES : (k + 1) * LANES] = jnp.concatenate(
                [r0, r1, r0, r1, r2, r0], axis=0
            ).astype(jnp.bfloat16)
            cvs[k] = jnp.broadcast_to(cv_v[pl.ds(b, 1), :], (8, LANES))
            scale = norm * cw_v[pl.ds(b, 1), :]
            table_ref[e] = scale * jnp.concatenate([one, m], axis=0)
            sums[k] = jnp.zeros((8, LANES), jnp.float32)
        for h in range(LANES // SUB):

            @pl.when(n_live > h * SUB)
            def _():
                left_rows = lhs_s[h * SUB : (h + 1) * SUB, :48]
                for k in range(0, listed, 2):
                    both = jnp.dot(
                        left_rows, rhs_s[:, k * LANES : (k + 2) * LANES],
                        preferred_element_type=jnp.float32,
                    )
                    for n in range(2):
                        total = sums[k + n]
                        cv = cvs[k + n]
                        for q in range(0, SUB, 8):
                            rows = slice(h * SUB + q, h * SUB + q + 8)
                            root = lax.rsqrt(avb[rows, :] + cv)
                            inv = root * root
                            ex = jnp.exp2(both[q : q + 8, n * LANES : (n + 1) * LANES] * inv)
                            ov = (root * inv) * (ex * wb[rows, :])
                            g_buf[turn, h, (k + n) * SUB + q : (k + n) * SUB + q + 8, :] = ov * inv
                            total = total + ov
                        sums[k + n] = total
                out_copy(a, h).start()

        for k in range(listed):
            e = a * listed + k
            partial = jnp.sum(sums[k], axis=0, keepdims=True) * table_ref[e][0:1]
            place = owner[lst[e]]
            dev = lax.div(place, owned)
            slot = place - dev * owned
            rank = count[dev]
            count[dev] = rank + 1
            pos_ref[e] = dev * CAPACITY + rank
            send_ref[dev, pl.ds(rank, 1), :] = partial
            before = send_ref[dev, CAPACITY : CAPACITY + 1, :]
            send_ref[dev, CAPACITY : CAPACITY + 1, :] = jnp.where(
                lane == rank, slot.astype(jnp.float32), before
            )
        return carry

    lax.fori_loop(0, blocks, block, 0)
    for last in range(max(0, blocks - OUT_SLOTS), blocks):
        drain(last)


def force_kernel(
    listed, pos_h, live_h, x_h, g_h, ret_ref, table_ref, mean_v, f_ref, mean_h,
    g_buf, g_sems, pos, live, x_v, coef, sums, sems,
):
    blocks = live.shape[0]
    loads = [
        pltpu.make_async_copy(src, dst, sems.at[i])
        for i, (src, dst) in enumerate([(pos_h, pos), (live_h, live), (x_h, x_v), (mean_v, mean_h)])
    ]
    for load in loads:
        load.start()
    for load in loads[:3]:
        load.wait()
    ones = jnp.ones((8, LANES), jnp.float32)

    def in_copy(a, h):
        turn = lax.rem(a, IN_SLOTS)
        return pltpu.make_async_copy(g_h.at[a, h], g_buf.at[turn, h], g_sems.at[turn, h])

    def fetch(a):
        for h in range(LANES // SUB):

            @pl.when(live[a] > h * SUB)
            def _():
                in_copy(a, h).start()

    for first in range(min(IN_SLOTS - 1, blocks)):
        fetch(first)

    def block(a, carry):
        n_live = live[a]
        turn = lax.rem(a, IN_SLOTS)

        @pl.when(a + IN_SLOTS - 1 < blocks)
        def _():
            fetch(a + IN_SLOTS - 1)

        for k in range(listed):
            e = a * listed + k
            scale = energy_unit * ret_ref[pl.ds(pos[e], 1), :]
            rows = table_ref[e] * scale
            for c in range(4):
                coef[k, c] = jnp.broadcast_to(rows[c : c + 1], (8, LANES))
        for h in range(LANES // SUB):

            @pl.when(n_live > h * SUB)
            def _():
                in_copy(a, h).wait()
                acc = [[jnp.zeros((8, LANES), jnp.float32) for _ in range(SUB // 8)] for _ in range(4)]
                for k in range(listed):
                    for q in range(SUB // 8):
                        g = g_buf[turn, h, k * SUB + q * 8 : k * SUB + q * 8 + 8, :]
                        for c in range(4):
                            acc[c][q] = acc[c][q] + g * coef[k, c]
                for c in range(4):
                    for q in range(SUB // 8):
                        sums[c, h * SUB + q * 8 : h * SUB + q * 8 + 8, :] = acc[c][q]

            @pl.when(n_live <= h * SUB)
            def _():
                sums[:, h * SUB : (h + 1) * SUB, :] = jnp.zeros((4, SUB, LANES), jnp.float32)

        flat = [
            lax.dot_general(
                ones, sums[c], (((1,), (1,)), ((), ())), precision=lax.Precision.HIGHEST,
                preferred_element_type=jnp.float32,
            )[0:1]
            for c in range(4)
        ]
        here = pl.ds(pl.multiple_of(a * LANES, LANES), LANES)
        for c in range(3):
            f_ref[c, :, here] = x_v[c, :, here] * flat[0] - flat[c + 1]
        return carry

    lax.fori_loop(0, blocks, block, 0)
    loads[3].wait()


def exchange_kernel(
    domains, replicas, send_ref, target_h, sigma_h, mean_ref, ret_ref,
    target_ref, sigma_ref, loads, got, acc, part, back, land, out_send, out_recv, rep_send, rep_recv, back_send, back_recv,
):
    me_d = lax.axis_index("dom")
    me_r = lax.axis_index("rep")
    owned = target_ref.shape[0]
    stages = replicas.bit_length() - 1
    partners = []
    for t in range(stages):
        bit = 1 << t
        partners.append(me_r + bit - 2 * bit * lax.rem(lax.div(me_r, bit), 2))
    fetches = [
        pltpu.make_async_copy(target_h, target_ref, loads.at[0]),
        pltpu.make_async_copy(sigma_h, sigma_ref, loads.at[1]),
    ]
    for fetch in fetches:
        fetch.start()
    barrier = pltpu.get_barrier_semaphore()
    for s in range(1, domains):
        pl.semaphore_signal(
            barrier, inc=1, device_id=(me_r, lax.rem(me_d + s, domains)), device_id_type=MESH
        )
    for t in range(stages):
        pl.semaphore_signal(barrier, inc=1, device_id=(partners[t], me_d), device_id_type=MESH)
    pl.semaphore_wait(barrier, domains - 1 + stages)

    outs = [None]
    for s in range(1, domains):
        peer = lax.rem(me_d + s, domains)
        copy = pltpu.make_async_remote_copy(
            src_ref=send_ref.at[peer],
            dst_ref=got.at[s],
            send_sem=out_send.at[s],
            recv_sem=out_recv.at[s],
            device_id=(me_r, peer),
            device_id_type=MESH,
        )
        copy.start()
        outs.append(copy)

    row = lax.broadcasted_iota(jnp.int32, (owned, CAPACITY), 0).astype(jnp.float32)

    def picks_of(s):
        slots = (
            send_ref[me_d, CAPACITY : CAPACITY + 1, :] if s == 0 else got[s, CAPACITY : CAPACITY + 1, :]
        )
        return jnp.where(row == slots[:, :CAPACITY], 1.0, 0.0).astype(jnp.bfloat16)

    total = jnp.zeros((owned, LANES), jnp.float32)
    for s in range(domains):
        if s:
            outs[s].wait_recv()
        rows = send_ref[me_d, :CAPACITY, :] if s == 0 else got[s, :CAPACITY, :]
        picks = picks_of(s)
        for piece in three(rows):
            total = total + jnp.dot(picks, piece, preferred_element_type=jnp.float32)
    acc[0] = total
    swaps = []
    for t in range(stages):
        copy = pltpu.make_async_remote_copy(
            src_ref=acc.at[t],
            dst_ref=part.at[t],
            send_sem=rep_send.at[t],
            recv_sem=rep_recv.at[t],
            device_id=(partners[t], me_d),
            device_id_type=MESH,
        )
        copy.start()
        swaps.append(copy)
        copy.wait_recv()
        total = total + part[t]
        if t + 1 < stages:
            acc[t + 1] = total
    mean = total / replicas
    mean_ref[...] = mean
    for fetch in fetches:
        fetch.wait()
    misfit = mean - target_ref[...]
    sigmas = sigma_ref[...]
    adjoint = misfit / (sigmas * sigmas + 0.5 * misfit * misfit) / replicas
    pieces = three(adjoint)
    backs = []
    for s in list(range(1, domains)) + [0]:
        picks = picks_of(s)
        rows = jnp.zeros((CAPACITY, LANES), jnp.float32)
        for piece in pieces:
            rows = rows + lax.dot_general(
                picks, piece, (((0,), (0,)), ((), ())), preferred_element_type=jnp.float32
            )
        if s == 0:
            ret_ref[me_d] = rows
            continue
        back[s] = rows
        peer = lax.rem(me_d + domains - s, domains)
        copy = pltpu.make_async_remote_copy(
            src_ref=back.at[s],
            dst_ref=land.at[s],
            send_sem=back_send.at[s],
            recv_sem=back_recv.at[s],
            device_id=(me_r, peer),
            device_id_type=MESH,
        )
        copy.start()
        backs.append((s, copy))
    for s, copy in backs:
        copy.wait_recv()
        ret_ref[lax.rem(me_d + s, domains)] = land[s]
    for copy in outs[1:] + swaps + [copy for _, copy in backs]:
        copy.wait_send()


def shards(
    coords, atom_var, atom_weight, atoms_live, block_list, owner_map,
    comp_means, comp_var, comp_weight, target, noise_sigma,
):
    replicas = lax.axis_size("rep")
    domains = lax.axis_size("dom")
    blocks, listed = block_list.shape
    comp_blocks = owner_map.shape[0]
    owned = target.shape[0] // LANES
    entries = blocks * listed
    x = coords.transpose(1, 0, 2)
    lst = block_list.reshape(-1)
    cv = comp_var.reshape(comp_blocks, LANES)
    cw = comp_weight.reshape(comp_blocks, LANES)
    f32, i32, bf16 = jnp.float32, jnp.int32, jnp.bfloat16
    whole = pl.BlockSpec(memory_space=VMEM)
    far = pl.BlockSpec(memory_space=pltpu.HBM)
    send, pos, table, g = pl.pallas_call(
        functools.partial(pair_kernel, listed, owned),
        in_specs=[far] * 9,
        out_specs=[whole, pl.BlockSpec(memory_space=pltpu.SMEM), whole, far],
        out_shape=[
            jax.ShapeDtypeStruct((domains, ROWS, LANES), f32),
            jax.ShapeDtypeStruct((entries,), i32),
            jax.ShapeDtypeStruct((entries, 4, LANES), f32),
            jax.ShapeDtypeStruct((blocks, LANES // SUB, listed * SUB, LANES), f32),
        ],
        scratch_shapes=[
            VMEM((OUT_SLOTS, LANES // SUB, listed * SUB, LANES), f32),
            pltpu.SemaphoreType.DMA((OUT_SLOTS, LANES // SUB)),
            pltpu.SMEM((blocks,), i32),
            pltpu.SMEM((entries,), i32),
            pltpu.SMEM((comp_blocks,), i32),
            VMEM(x.shape, f32),
            VMEM((blocks, LANES), f32),
            VMEM((blocks, LANES), f32),
            VMEM(comp_means.shape, f32),
            VMEM(cv.shape, f32),
            VMEM(cw.shape, f32),
            pltpu.SMEM((domains,), i32),
            VMEM((LANES, LANES), f32),
            VMEM((LANES, LANES), f32),
            VMEM((LANES, LANES), bf16),
            VMEM((48, listed * LANES), bf16),
            VMEM((listed, 8, LANES), f32),
            VMEM((listed, 8, LANES), f32),
            pltpu.SemaphoreType.DMA((9,)),
        ],
        compiler_params=pltpu.CompilerParams(vmem_limit_bytes=57 << 20),
        name="pairs",
    )(
        atoms_live, lst, owner_map, x,
        atom_var.reshape(blocks, LANES), atom_weight.reshape(blocks, LANES),
        comp_means, cv, cw,
    )
    stages = replicas.bit_length() - 1
    mean, ret = pl.pallas_call(
        functools.partial(exchange_kernel, domains, replicas),
        in_specs=[whole, far, far],
        out_specs=[whole] * 2,
        out_shape=[
            jax.ShapeDtypeStruct((owned, LANES), f32),
            jax.ShapeDtypeStruct((domains, CAPACITY, LANES), f32),
        ],
        scratch_shapes=[
            VMEM((owned, LANES), f32),
            VMEM((owned, LANES), f32),
            pltpu.SemaphoreType.DMA((2,)),
            VMEM((domains, ROWS, LANES), f32),
            VMEM((stages, owned, LANES), f32),
            VMEM((stages, owned, LANES), f32),
            VMEM((domains, CAPACITY, LANES), f32),
            VMEM((domains, CAPACITY, LANES), f32),
            pltpu.SemaphoreType.DMA((domains,)),
            pltpu.SemaphoreType.DMA((domains,)),
            pltpu.SemaphoreType.DMA((stages,)),
            pltpu.SemaphoreType.DMA((stages,)),
            pltpu.SemaphoreType.DMA((domains,)),
            pltpu.SemaphoreType.DMA((domains,)),
        ],
        compiler_params=pltpu.CompilerParams(
            collective_id=0, has_side_effects=True, vmem_limit_bytes=57 << 20
        ),
        name="exchange",
    )(send, target.reshape(owned, LANES), noise_sigma.reshape(owned, LANES))
    forces, mean = pl.pallas_call(
        functools.partial(force_kernel, listed),
        in_specs=[pl.BlockSpec(memory_space=pl.ANY), far, far, far, whole, whole, whole],
        out_specs=[whole, far],
        out_shape=[
            jax.ShapeDtypeStruct(x.shape, f32),
            jax.ShapeDtypeStruct((owned, LANES), f32),
        ],
        scratch_shapes=[
            VMEM((IN_SLOTS, LANES // SUB, listed * SUB, LANES), f32),
            pltpu.SemaphoreType.DMA((IN_SLOTS, LANES // SUB)),
            pltpu.SMEM((entries,), i32),
            pltpu.SMEM((blocks,), i32),
            VMEM(x.shape, f32),
            VMEM((listed, 4, 8, LANES), f32),
            VMEM((4, LANES, LANES), f32),
            pltpu.SemaphoreType.DMA((4,)),
        ],
        compiler_params=pltpu.CompilerParams(vmem_limit_bytes=57 << 20),
        name="forces",
    )(pos, atoms_live, x, g, ret.reshape(domains * CAPACITY, LANES), table, mean)
    return (mean.reshape(-1), forces.transpose(1, 0, 2))


def solution(mesh):
    return jax.shard_map(
        shards,
        mesh=mesh,
        in_specs=(
            P("rep", None, "dom"),
            P("dom"),
            P("dom"),
            P("dom"),
            P("dom", None),
            P(),
            P(),
            P(),
            P(),
            P("dom"),
            P("dom"),
        ),
        out_specs=(P("dom"), P("rep", None, "dom")),
        check_vma=False,
    )
```

time: 106 us -> 105 us (level)
  local copies, waits for them, and re-layouts: 15.7 us -> 1.43 us
  Pallas kernels: 88.6 us -> 102 us
    unnamed x26 -> x1, local copies, waits for them, and re-layouts: 15.6 us -> 0.77 us
    pallas_call x2, Pallas kernels: 60 us -> 71.6 us  [the longest x1 37.2 us: shards(): pl.pallas_call(functools.partial(pair_kernel, listed, owned), in_specs=[f...]
    pallas_call x1, Pallas kernels: 28.6 us -> 30.7 us  [shards(): pl.pallas_call(functools.partial(exchange_kernel, domains, replicas), in_...]
where the time goes in v2:
time: 105 us; the launch traced here: 104 us
  Pallas kernels  102 us (97%)
  local copies, waits for them, and re-layouts  1.43 us (1%)
    pallas_call x1, Pallas kernels, shards(): pl.pallas_call(functools.partial(pair_kernel, listed, owned), in_specs=[f...  37.2 us
    pallas_call x1, Pallas kernels, shards(): pl.pallas_call(functools.partial(force_kernel, listed), in_specs=[pl.Bloc...  34.4 us
    pallas_call x1, Pallas kernels, shards(): pl.pallas_call(functools.partial(exchange_kernel, domains, replicas), in_...  30.7 us

profile of v2, /device:TPU:0, one launch (start us, length us, event | category | flops | bytes accessed | tf_op | source)
XLA Modules:
  0.0 104.4 jit_solution(5456007368895538572)
XLA Ops:
  0.6 0.8 copy.13
  1.4 0.7 reshape.31.lst_h
  2.1 37.2 %pairs.1 = (f32[8,72,128]{2,1,0:T(8,128)}, s32[512]{0:T(512)}, f32[512,4,128]{2,1,0:T(4,128)}, f32[32,4,512,128]{3,2,1,0:T(8,128)}) custom-call(s32[32]{0:T(128)} %live_h.3, s32[512]{0:T(512)} %reshape.31.lst_h, s32[2048]{0:T(1024)} %owner_h.1, f32[3,1,4096]{2,1,0:T(1,128)} %bitcast.13, f32[32,128]{1,0:T(8,128)} %bitcast.17, f32[32,128]{1,0:T(8,128)} %bitcast.18, ...), custom_call_target="tpu_custom_call" | custom-call | tf_op jit(solution)/shard_map/pairs/pallas_call | solution.py:360
  39.3 30.7 %exchange.1 = (f32[256,128]{1,0:T(8,128)}, f32[8,64,128]{2,1,0:T(8,128)}) custom-call(f32[8,72,128]{2,1,0:T(8,128)} %get-tuple-element.12.send_ref, f32[256,128]{1,0:T(8,128)} %bitcast.15, f32[256,128]{1,0:T(8,128)} %bitcast.16), custom_call_target="tpu_custom_call" | custom-call | tf_op jit(solution)/shard_map/exchange/pallas_call | solution.py:399
  70.1 34.4 %forces.1 = (f32[3,1,4096]{2,1,0:T(1,128)}, f32[256,128]{1,0:T(8,128)}) custom-call(s32[512]{0:T(512)} %get-tuple-element.10.pos_h, s32[32]{0:T(128)} %live_h.3, f32[3,1,4096]{2,1,0:T(1,128)} %bitcast.14, f32[32,4,512,128]{3,2,1,0:T(8,128)} %get-tuple-element.11.g_h, f32[512,128]{1,0:T(8,128)} %bitcast.12, f32[512,4,128]{2,1,0:T(4,128)} %get-tuple-element.14.table_ref, ...), custom_call_target="tpu_custom_call" | custom-call | tf_op jit(solution)/shard_map/forces/pallas_call | solution.py:428

commit v3 on v2

--- a/solution.py
+++ b/solution.py
@@ -12,6 +12,7 @@
 ROWS = CAPACITY + 8
 LANES = 128
 SUB = 32
+HALF = 16
 OUT_SLOTS = 3
 IN_SLOTS = 5
 
@@ -37,7 +38,7 @@
 def pair_kernel(
     listed, owned, live_h, lst_h, owner_h, x_h, av_h, aw_h, m_h, cv_h, cw_h,
     send_ref, pos_ref, table_ref, g_h,
-    g_buf, g_sems, live, lst, owner, x_v, av_v, aw_v, m_v, cv_v, cw_v, count, avb, wb, lhs_s, rhs_s, cvs, sums, sems,
+    g_buf, g_sems, live, lst, owner, x_v, av_v, aw_v, m_v, cv_v, cw_v, count, avb, wb, sems,
 ):
     domains = send_ref.shape[0]
     blocks = live.shape[0]
@@ -60,79 +61,50 @@
     one = jnp.ones((1, LANES), jnp.float32)
     none = jnp.zeros((3, LANES), jnp.float32)
 
-    def out_copy(a, h):
+    def out_copy(a):
         turn = lax.rem(a, OUT_SLOTS)
-        return pltpu.make_async_copy(g_buf.at[turn, h], g_h.at[a, h], g_sems.at[turn, h])
-
-    def drain(a):
-        for h in range(LANES // SUB):
-
-            @pl.when(live[a] > h * SUB)
-            def _():
-                out_copy(a, h).wait()
+        return pltpu.make_async_copy(g_buf.at[turn], g_h.at[a], g_sems.at[turn])
 
     def block(a, carry):
-        n_live = live[a]
         turn = lax.rem(a, OUT_SLOTS)
 
         @pl.when(a >= OUT_SLOTS)
         def _():
-            drain(a - OUT_SLOTS)
+            out_copy(a - OUT_SLOTS).wait()
 
         x = jnp.concatenate(
             [x_v[c, :, pl.ds(pl.multiple_of(a * LANES, LANES), LANES)] for c in range(3)], axis=0
         )
-        weights = jnp.where(lane < n_live, aw_v[pl.ds(a, 1), :], 0.0)
+        weights = jnp.where(lane < live[a], aw_v[pl.ds(a, 1), :], 0.0)
         avb[...] = jnp.transpose(jnp.broadcast_to(av_v[pl.ds(a, 1), :], (LANES, LANES)))
         wb[...] = jnp.transpose(jnp.broadcast_to(weights, (LANES, LANES)))
         xx = jnp.sum(x * x, axis=0, keepdims=True)
         left = half_log2e * jnp.concatenate([-2.0 * x, one, xx, none], axis=0)
         l0, l1, l2 = three_f32(left)
-        pad = jnp.zeros((LANES - 48, LANES), jnp.float32)
-        lhs_s[...] = jnp.transpose(jnp.concatenate([l0, l0, l1, l1, l0, l2, pad], axis=0)).astype(
-            jnp.bfloat16
-        )
+        lhs = jnp.concatenate([l0, l0, l1, l1, l0, l2], axis=0).astype(jnp.bfloat16)
         for k in range(listed):
             e = a * listed + k
             b = lst[e]
             m = m_v[:, pl.ds(pl.multiple_of(b * LANES, LANES), LANES)]
             mm = jnp.sum(m * m, axis=0, keepdims=True)
             r0, r1, r2 = three_f32(jnp.concatenate([m, mm, one, none], axis=0))
-            rhs_s[:, k * LANES : (k + 1) * LANES] = jnp.concatenate(
-                [r0, r1, r0, r1, r2, r0], axis=0
-            ).astype(jnp.bfloat16)
-            cvs[k] = jnp.broadcast_to(cv_v[pl.ds(b, 1), :], (8, LANES))
+            rhs = jnp.concatenate([r0, r1, r0, r1, r2, r0], axis=0).astype(jnp.bfloat16)
+            scaled = lax.dot_general(
+                lhs, rhs, (((0,), (0,)), ((), ())), preferred_element_type=jnp.float32
+            )
+            cv = cv_v[pl.ds(b, 1), :]
+            total = jnp.zeros((SUB, LANES), jnp.float32)
+            for h in range(LANES // SUB):
+                rows = slice(h * SUB, (h + 1) * SUB)
+                root = lax.rsqrt(avb[rows, :] + cv)
+                inv = root * root
+                ov = (root * inv) * jnp.exp2(scaled[rows] * inv) * wb[rows, :]
+                g_buf[turn, k * LANES + h * SUB : k * LANES + (h + 1) * SUB, :] = ov * inv
+                total = total + ov
             scale = norm * cw_v[pl.ds(b, 1), :]
             table_ref[e] = scale * jnp.concatenate([one, m], axis=0)
-            sums[k] = jnp.zeros((8, LANES), jnp.float32)
-        for h in range(LANES // SUB):
-
-            @pl.when(n_live > h * SUB)
-            def _():
-                left_rows = lhs_s[h * SUB : (h + 1) * SUB, :48]
-                for k in range(0, listed, 2):
-                    both = jnp.dot(
-                        left_rows, rhs_s[:, k * LANES : (k + 2) * LANES],
-                        preferred_element_type=jnp.float32,
-                    )
-                    for n in range(2):
-                        total = sums[k + n]
-                        cv = cvs[k + n]
-                        for q in range(0, SUB, 8):
-                            rows = slice(h * SUB + q, h * SUB + q + 8)
-                            root = lax.rsqrt(avb[rows, :] + cv)
-                            inv = root * root
-                            ex = jnp.exp2(both[q : q + 8, n * LANES : (n + 1) * LANES] * inv)
-                            ov = (root * inv) * (ex * wb[rows, :])
-                            g_buf[turn, h, (k + n) * SUB + q : (k + n) * SUB + q + 8, :] = ov * inv
-                            total = total + ov
-                        sums[k + n] = total
-                out_copy(a, h).start()
-
-        for k in range(listed):
-            e = a * listed + k
-            partial = jnp.sum(sums[k], axis=0, keepdims=True) * table_ref[e][0:1]
-            place = owner[lst[e]]
+            partial = jnp.sum(total, axis=0, keepdims=True) * scale
+            place = owner[b]
             dev = lax.div(place, owned)
             slot = place - dev * owned
             rank = count[dev]
@@ -143,75 +115,61 @@
             send_ref[dev, CAPACITY : CAPACITY + 1, :] = jnp.where(
                 lane == rank, slot.astype(jnp.float32), before
             )
+        out_copy(a).start()
         return carry
 
     lax.fori_loop(0, blocks, block, 0)
     for last in range(max(0, blocks - OUT_SLOTS), blocks):
-        drain(last)
+        out_copy(last).wait()
 
 
 def force_kernel(
-    listed, pos_h, live_h, x_h, g_h, ret_ref, table_ref, mean_v, f_ref, mean_h,
-    g_buf, g_sems, pos, live, x_v, coef, sums, sems,
+    listed, pos_h, x_h, g_h, ret_ref, table_ref, mean_v, f_ref, mean_h,
+    g_buf, g_sems, pos, x_v, coef, sums, sems,
 ):
-    blocks = live.shape[0]
+    blocks = x_v.shape[2] // LANES
     loads = [
         pltpu.make_async_copy(src, dst, sems.at[i])
-        for i, (src, dst) in enumerate([(pos_h, pos), (live_h, live), (x_h, x_v), (mean_v, mean_h)])
+        for i, (src, dst) in enumerate([(pos_h, pos), (x_h, x_v), (mean_v, mean_h)])
     ]
     for load in loads:
         load.start()
-    for load in loads[:3]:
+    for load in loads[:2]:
         load.wait()
     ones = jnp.ones((8, LANES), jnp.float32)
 
-    def in_copy(a, h):
+    def in_copy(a):
         turn = lax.rem(a, IN_SLOTS)
-        return pltpu.make_async_copy(g_h.at[a, h], g_buf.at[turn, h], g_sems.at[turn, h])
-
-    def fetch(a):
-        for h in range(LANES // SUB):
-
-            @pl.when(live[a] > h * SUB)
-            def _():
-                in_copy(a, h).start()
+        return pltpu.make_async_copy(g_h.at[a], g_buf.at[turn], g_sems.at[turn])
 
     for first in range(min(IN_SLOTS - 1, blocks)):
-        fetch(first)
+        in_copy(first).start()
 
     def block(a, carry):
-        n_live = live[a]
         turn = lax.rem(a, IN_SLOTS)
 
         @pl.when(a + IN_SLOTS - 1 < blocks)
         def _():
-            fetch(a + IN_SLOTS - 1)
-
+            in_copy(a + IN_SLOTS - 1).start()
+
+        in_copy(a).wait()
         for k in range(listed):
             e = a * listed + k
             scale = energy_unit * ret_ref[pl.ds(pos[e], 1), :]
             rows = table_ref[e] * scale
             for c in range(4):
                 coef[k, c] = jnp.broadcast_to(rows[c : c + 1], (8, LANES))
-        for h in range(LANES // SUB):
-
-            @pl.when(n_live > h * SUB)
-            def _():
-                in_copy(a, h).wait()
-                acc = [[jnp.zeros((8, LANES), jnp.float32) for _ in range(SUB // 8)] for _ in range(4)]
-                for k in range(listed):
-                    for q in range(SUB // 8):
-                        g = g_buf[turn, h, k * SUB + q * 8 : k * SUB + q * 8 + 8, :]
-                        for c in range(4):
-                            acc[c][q] = acc[c][q] + g * coef[k, c]
-                for c in range(4):
-                    for q in range(SUB // 8):
-                        sums[c, h * SUB + q * 8 : h * SUB + q * 8 + 8, :] = acc[c][q]
-
-            @pl.when(n_live <= h * SUB)
-            def _():
-                sums[:, h * SUB : (h + 1) * SUB, :] = jnp.zeros((4, SUB, LANES), jnp.float32)
-
+        for h in range(LANES // HALF):
+            acc = [[jnp.zeros((8, LANES), jnp.float32) for _ in range(HALF // 8)] for _ in range(4)]
+            for k in range(listed):
+                for q in range(HALF // 8):
+                    start = k * LANES + h * HALF + q * 8
+                    g = g_buf[turn, start : start + 8, :]
+                    for c in range(4):
+                        acc[c][q] = acc[c][q] + g * coef[k, c]
+            for c in range(4):
+                for q in range(HALF // 8):
+                    sums[c, h * HALF + q * 8 : h * HALF + q * 8 + 8, :] = acc[c][q]
         flat = [
             lax.dot_general(
                 ones, sums[c], (((1,), (1,)), ((), ())), precision=lax.Precision.HIGHEST,
@@ -225,7 +183,7 @@
         return carry
 
     lax.fori_loop(0, blocks, block, 0)
-    loads[3].wait()
+    loads[2].wait()
 
 
 def exchange_kernel(
@@ -354,7 +312,7 @@
     lst = block_list.reshape(-1)
     cv = comp_var.reshape(comp_blocks, LANES)
     cw = comp_weight.reshape(comp_blocks, LANES)
-    f32, i32, bf16 = jnp.float32, jnp.int32, jnp.bfloat16
+    f32, i32 = jnp.float32, jnp.int32
     whole = pl.BlockSpec(memory_space=VMEM)
     far = pl.BlockSpec(memory_space=pltpu.HBM)
     send, pos, table, g = pl.pallas_call(
@@ -365,11 +323,11 @@
             jax.ShapeDtypeStruct((domains, ROWS, LANES), f32),
             jax.ShapeDtypeStruct((entries,), i32),
             jax.ShapeDtypeStruct((entries, 4, LANES), f32),
-            jax.ShapeDtypeStruct((blocks, LANES // SUB, listed * SUB, LANES), f32),
+            jax.ShapeDtypeStruct((blocks, listed * LANES, LANES), f32),
         ],
         scratch_shapes=[
-            VMEM((OUT_SLOTS, LANES // SUB, listed * SUB, LANES), f32),
-            pltpu.SemaphoreType.DMA((OUT_SLOTS, LANES // SUB)),
+            VMEM((OUT_SLOTS, listed * LANES, LANES), f32),
+            pltpu.SemaphoreType.DMA((OUT_SLOTS,)),
             pltpu.SMEM((blocks,), i32),
             pltpu.SMEM((entries,), i32),
             pltpu.SMEM((comp_blocks,), i32),
@@ -382,10 +340,6 @@
             pltpu.SMEM((domains,), i32),
             VMEM((LANES, LANES), f32),
             VMEM((LANES, LANES), f32),
-            VMEM((LANES, LANES), bf16),
-            VMEM((48, listed * LANES), bf16),
-            VMEM((listed, 8, LANES), f32),
-            VMEM((listed, 8, LANES), f32),
             pltpu.SemaphoreType.DMA((9,)),
         ],
         compiler_params=pltpu.CompilerParams(vmem_limit_bytes=57 << 20),
@@ -427,25 +381,24 @@
     )(send, target.reshape(owned, LANES), noise_sigma.reshape(owned, LANES))
     forces, mean = pl.pallas_call(
         functools.partial(force_kernel, listed),
-        in_specs=[pl.BlockSpec(memory_space=pl.ANY), far, far, far, whole, whole, whole],
+        in_specs=[pl.BlockSpec(memory_space=pl.ANY), far, far, whole, whole, whole],
         out_specs=[whole, far],
         out_shape=[
             jax.ShapeDtypeStruct(x.shape, f32),
             jax.ShapeDtypeStruct((owned, LANES), f32),
         ],
         scratch_shapes=[
-            VMEM((IN_SLOTS, LANES // SUB, listed * SUB, LANES), f32),
-            pltpu.SemaphoreType.DMA((IN_SLOTS, LANES // SUB)),
+            VMEM((IN_SLOTS, listed * LANES, LANES), f32),
+            pltpu.SemaphoreType.DMA((IN_SLOTS,)),
             pltpu.SMEM((entries,), i32),
-            pltpu.SMEM((blocks,), i32),
             VMEM(x.shape, f32),
             VMEM((listed, 4, 8, LANES), f32),
             VMEM((4, LANES, LANES), f32),
-            pltpu.SemaphoreType.DMA((4,)),
+            pltpu.SemaphoreType.DMA((3,)),
         ],
         compiler_params=pltpu.CompilerParams(vmem_limit_bytes=57 << 20),
         name="forces",
-    )(pos, atoms_live, x, g, ret.reshape(domains * CAPACITY, LANES), table, mean)
+    )(pos, x, g, ret.reshape(domains * CAPACITY, LANES), table, mean)
     return (mean.reshape(-1), forces.transpose(1, 0, 2))
 
 

time: 105 us -> 83.3 us (0.79)
  Pallas kernels: 102 us -> 80.9 us
    pallas_call x1, Pallas kernels: 37.2 us -> 23.9 us  [shards(): pl.pallas_call(functools.partial(pair_kernel, listed, owned), in_specs=[f...]
    pallas_call x1, Pallas kernels: 34.4 us -> 26.7 us  [shards(): pl.pallas_call(functools.partial(force_kernel, listed), in_specs=[pl.Bloc...]
where the time goes in v3:
time: 83.3 us; the launch traced here: 83 us
  Pallas kernels  80.9 us (97%)
  local copies, waits for them, and re-layouts  1.43 us (2%)
    pallas_call x1, Pallas kernels, shards(): pl.pallas_call(functools.partial(exchange_kernel, domains, replicas), in_...  30.4 us
    pallas_call x1, Pallas kernels, shards(): pl.pallas_call(functools.partial(force_kernel, listed), in_specs=[pl.Bloc...  26.7 us
    pallas_call x1, Pallas kernels, shards(): pl.pallas_call(functools.partial(pair_kernel, listed, owned), in_specs=[f...  23.9 us

profile of v3, /device:TPU:0, one launch (start us, length us, event | category | flops | bytes accessed | tf_op | source)
XLA Modules:
  0.0 83.0 jit_solution(13300255094726223002)
XLA Ops:
  0.6 0.8 copy.13
  1.4 0.7 reshape.31.lst_h
  2.1 23.9 %pairs.1 = (f32[8,72,128]{2,1,0:T(8,128)}, s32[512]{0:T(512)}, f32[512,4,128]{2,1,0:T(4,128)}, f32[32,2048,128]{2,1,0:T(8,128)}) custom-call(s32[32]{0:T(128)} %live_h.1, s32[512]{0:T(512)} %reshape.31.lst_h, s32[2048]{0:T(1024)} %owner_h.1, f32[3,1,4096]{2,1,0:T(1,128)} %bitcast.13, f32[32,128]{1,0:T(8,128)} %bitcast.17, f32[32,128]{1,0:T(8,128)} %bitcast.18, ...), custom_call_target="tpu_custom_call" | custom-call | tf_op jit(solution)/shard_map/pairs/pallas_call | solution.py:318
  25.9 30.4 %exchange.1 = (f32[256,128]{1,0:T(8,128)}, f32[8,64,128]{2,1,0:T(8,128)}) custom-call(f32[8,72,128]{2,1,0:T(8,128)} %get-tuple-element.12.send_ref, f32[256,128]{1,0:T(8,128)} %bitcast.15, f32[256,128]{1,0:T(8,128)} %bitcast.16), custom_call_target="tpu_custom_call" | custom-call | tf_op jit(solution)/shard_map/exchange/pallas_call | solution.py:353
  56.3 26.7 %forces.1 = (f32[3,1,4096]{2,1,0:T(1,128)}, f32[256,128]{1,0:T(8,128)}) custom-call(s32[512]{0:T(512)} %get-tuple-element.10.pos_h, f32[3,1,4096]{2,1,0:T(1,128)} %bitcast.14, f32[32,2048,128]{2,1,0:T(8,128)} %get-tuple-element.11.g_h, f32[512,128]{1,0:T(8,128)} %bitcast.12, f32[512,4,128]{2,1,0:T(4,128)} %get-tuple-element.14.table_ref, ...), custom_call_target="tpu_custom_call" | custom-call | tf_op jit(solution)/shard_map/forces/pallas_call | solution.py:382
